TPU v7x, 128 devices: a whole 4x4x4 slice. The times are simulated.
128 devices in a mesh: wide: 32 (over z, y_hi, x), narrow: 4 (over y_lo, core).
Axes of the slice: x: 4, y: 4 (y_hi: 2, y_lo: 2; y = y_hi * 2 + y_lo), z: 4, core: 2. Of those that a mesh axis runs over, the one named last changes fastest.
Arguments:
- spectra: bfloat16 [2, 128, 64, 32, 256], P(None, ('wide', 'narrow')), may hold values from -6 to 6
- out_grads: bfloat16 [2, 128, 64, 32, 256], P(None, ('wide', 'narrow')), may hold values from -0.375 to 0.375
- weights: float32 [2, 64, 32, 256, 256], P(None, 'wide', 'narrow'), may hold values from -6 to 6
- mode_factor: float32 [64, 8], replicated, may hold values from -2 to 2
- in_factor: float32 [256, 64], replicated, may hold values from -0.75 to 0.75
- out_factor: float32 [256, 64], replicated, may hold values from -0.75 to 0.75
- first_moment: float32 [2, 8, 32, 4096], P(None, None, 'narrow', 'wide'), may hold values from -60 to 60
- second_moment: float32 [8, 32, 4096], P(None, 'narrow', 'wide'), may hold values from 20 to 500
Outputs:
- new_weights: float32 [2, 64, 32, 256, 256], P(None, 'wide', 'narrow')
- new_first: float32 [2, 8, 32, 4096], P(None, None, 'narrow', 'wide')
- new_second: float32 [8, 32, 4096], P(None, 'narrow', 'wide')
All inputs are finite; a program needn't handle non-finite values.
Results may differ from a plain program's by a relative error of at most 0.0003.
Values may be sent and summed in bfloat16 or wider, within the bound.
No kernel may reach another device: no remote copies, remote signals or barrier semaphores. Data moves between devices by JAX's collectives and lax.ppermute only.
A program may use at most 128 MiB of HBM per device.

v0:
```python
import jax
import jax.numpy as jnp
from jax import lax
from jax.sharding import PartitionSpec as P

STEP = 1000
highest = lax.Precision.HIGHEST


def local(
    spectra, out_grads, weights, mode_factor, in_factor, out_factor, first_moment, second_moment
):
    wide_count = lax.axis_size("wide")
    narrow_count = lax.axis_size("narrow")
    modes_first = spectra.shape[2]
    modes_second = spectra.shape[3]
    channels = spectra.shape[4]
    first_mine = modes_first // wide_count
    second_mine = modes_second // narrow_count
    local_modes = first_mine * second_mine
    rank_in = in_factor.shape[1]
    rank_out = out_factor.shape[1]

    def arrange(source):
        sample_rows = source.shape[1]
        width = source.shape[4]
        source = source.reshape(
            2, sample_rows, wide_count, first_mine, narrow_count, second_mine, width
        )
        source = source.transpose(0, 1, 2, 4, 3, 5, 6)
        return source.reshape(2, sample_rows, wide_count * narrow_count * local_modes, width)

    mine_spectra, mine_grads = (
        lax.all_to_all(
            arrange(spectra), ("wide", "narrow"), split_axis=2, concat_axis=1, tiled=True
        ),
        lax.all_to_all(
            arrange(out_grads), ("wide", "narrow"), split_axis=2, concat_axis=1, tiled=True
        ),
    )
    products = jnp.einsum(
        "pbmi,qbmo->pqmio", mine_spectra, mine_grads, preferred_element_type=jnp.float32
    )
    grad = jnp.stack([products[0, 0] + products[1, 1], products[0, 1] - products[1, 0]])
    half_core = jnp.einsum("pmio,oc->pmic", grad, out_factor, precision=highest)
    channel_core = jnp.einsum("ia,pmic->pmac", in_factor, half_core, precision=highest)
    channel_core = channel_core.reshape(2, first_mine, second_mine, rank_in * rank_out)
    wide_position = lax.axis_index("wide")
    mine_rows = lax.dynamic_slice_in_dim(mode_factor, wide_position * first_mine, first_mine, 0)
    partial_core = jnp.einsum("xr,pxmk->prmk", mine_rows, channel_core, precision=highest)
    core_grad = lax.psum_scatter(partial_core, "wide", scatter_dimension=3, tiled=True)
    new_first = 0.9 * first_moment + 0.1 * core_grad
    new_second = 0.999 * second_moment + 0.001 * (
        core_grad[0] * core_grad[0] + core_grad[1] * core_grad[1]
    )
    first_scale = 1.0 / (1.0 - 0.9**STEP)
    second_scale = 1.0 / (1.0 - 0.999**STEP)
    core_step = new_first * first_scale / (jnp.sqrt(new_second * second_scale) + 1e-08)
    expanded = jnp.einsum(
        "xr,prmk->pxmk",
        mine_rows,
        lax.all_gather(core_step, "wide", axis=3, tiled=True),
        precision=highest,
    )
    expanded = expanded.reshape(2, local_modes, rank_in, rank_out)
    left_part = jnp.einsum("pmac,oc->pmao", expanded, out_factor, precision=highest)
    change = jnp.einsum("ia,pmao->pmio", in_factor, left_part, precision=highest)
    change = change.reshape(2, first_mine, second_mine, channels, channels)
    new_weights = weights - 0.3 * change
    return (new_weights, new_first, new_second)


def solution(mesh):
    placed = (
        P(None, ("wide", "narrow"), None, None, None),
        P(None, ("wide", "narrow"), None, None, None),
        P(None, "wide", "narrow", None, None),
        P(),
        P(),
        P(),
        P(None, None, "narrow", "wide"),
        P(None, "narrow", "wide"),
    )
    return jax.shard_map(
        local,
        mesh=mesh,
        in_specs=placed,
        out_specs=(
            P(None, "wide", "narrow", None, None),
            P(None, None, "narrow", "wide"),
            P(None, "narrow", "wide"),
        ),
        check_vma=False,
    )
```

profile of v0, /device:TPU:0, one launch (start us, length us, event | category | flops | bytes accessed | tf_op | source)
XLA Modules:
  0.0 412.7 jit_solution(15778321747352976225)
XLA Ops:
  7.2 1.8 copy.52
  9.0 14.0 %copy.53 = bf16[2,1,2048,256]{3,0,1,2:T(2,128)(2,1)} copy(bf16[2,1,2048,256]{3,2,0,1:T(8,128)(2,1)S(1)} %bitcast.77) | data formatting | bytes 4194304 | tf_op jit(solution)/shard_map/reshape | solution.py:31
  23.0 11.2 %all-to-all-start.1 = ((bf16[2,1,2048,256]{3,0,1,2:T(2,128)(2,1)}), bf16[2,1,2048,256]{3,0,1,2:T(2,128)(2,1)S(1)}, u32[]{:S(2)}, u32[]{:S(2)}) async-start(bf16[2,1,2048,256]{3,0,1,2:T(2,128)(2,1)} %copy.53), calls=%async_computation.1 | async-start | bytes 4194304 | tf_op jit(solution)/shard_map/all_to_all | solution.py:34
  34.2 1.8 copy.49
  36.0 14.0 %copy.50 = bf16[2,1,2048,256]{3,0,1,2:T(2,128)(2,1)} copy(bf16[2,1,2048,256]{3,2,0,1:T(8,128)(2,1)S(1)} %bitcast.78) | data formatting | bytes 4194304 | tf_op jit(solution)/shard_map/reshape | solution.py:31
  49.9 14.4 %all-to-all-done.1 = bf16[2,1,2048,256]{3,0,1,2:T(2,128)(2,1)S(1)} async-done(((bf16[2,1,2048,256]{3,0,1,2:T(2,128)(2,1)}), bf16[2,1,2048,256]{3,0,1,2:T(2,128)(2,1)S(1)}, u32[]{:S(2)}, u32[]{:S(2)}) %all-to-all-start.1) | async-done | bytes 2097184 | tf_op jit(solution)/shard_map/all_to_all | solution.py:34
  64.3 5.8 %all-to-all-start = ((bf16[2,1,2048,256]{3,0,1,2:T(2,128)(2,1)}), bf16[2,1,2048,256]{3,0,1,2:T(2,128)(2,1)}, u32[]{:S(2)}, u32[]{:S(2)}) async-start(bf16[2,1,2048,256]{3,0,1,2:T(2,128)(2,1)} %copy.50), calls=%async_computation | async-start | bytes 4194304 | tf_op jit(solution)/shard_map/all_to_all | solution.py:37
  70.1 0.2 reduce-scatter.2.cloned.1.call-start
  70.3 29.5 %all-to-all-done = bf16[2,1,2048,256]{3,0,1,2:T(2,128)(2,1)} async-done(((bf16[2,1,2048,256]{3,0,1,2:T(2,128)(2,1)}), bf16[2,1,2048,256]{3,0,1,2:T(2,128)(2,1)}, u32[]{:S(2)}, u32[]{:S(2)}) %all-to-all-start) | async-done | bytes 2097184 | tf_op jit(solution)/shard_map/all_to_all | solution.py:37
  99.8 7.4 %convolution_bitcast_fusion = f32[2,2,16,256,256]{3,4,0,1,2:T(8,128)S(1)} fusion(bf16[2,128,16,256,1]{3,0,2,1,4:T(2,128)(2,1)S(1)} %bitcast.76, bf16[2,128,16,256,1]{3,0,2,1,4:T(2,128)(2,1)} %bitcast.4), kind=kOutput, calls=%fused_computation | convolution fusion | flops 1073741824 | bytes 20971520 | tf_op jit(solution)/shard_map/pbmi,qbmo->pqmio/dot_general | solution.py:41
  107.2 0.6 fusion.4
  107.8 0.6 fusion.6
  108.4 0.2 copy-done.1
  108.6 5.6 %fusion = f32[2,16,256,64]{2,3,1,0:T(8,128)S(1)} fusion(f32[1,16,256,256]{2,3,1,0:T(8,128)S(1)} %fusion.4, f32[1,16,256,256]{2,3,1,0:T(8,128)S(1)} %fusion.6, f32[256,64]{0,1:T(8,128)S(1)} %copy-done.1), kind=kOutput, calls=%fused_computation.1 | convolution fusion | flops 1612709888 | bytes 10551296 | tf_op jit(solution)/shard_map/pmio,oc->pmic/dot_general | solution.py:45
  114.2 2.0 convolution_bitcast_fusion.3
  116.3 0.3 copy.60
  116.6 0.4 reshape.79
  117.0 3.5 convolution_bitcast_fusion.1
  120.6 0.0 all-gather.2.cloned.1.call-start
  120.6 185.0 %reduce-scatter.2.cloned.1.call-done = f32[2,8,8,128]{3,1,2,0:T(8,128)} async-done(((f32[2,8,8,4096]{3,1,2,0:T(8,128)}), f32[2,8,8,128]{3,1,2,0:T(8,128)}) %reduce-scatter.2.cloned.1.call-update) | async-done | bytes 65552 | tf_op jit(solution)/shard_map/reduce_scatter | solution.py:51
  305.6 0.8 sqrt_add_fusion
  306.5 1.5 broadcast_divide_fusion
  308.0 0.6 copy.66
  308.6 0.6 copy.67
  309.2 62.1 %all-gather.2.cloned.1.call-done = f32[2,8,8,4096]{3,1,2,0:T(8,128)} async-done(((f32[2,8,8,128]{3,1,2,0:T(8,128)}), f32[2,8,8,4096]{3,1,2,0:T(8,128)}) %all-gather.2.cloned.1.call-update) | async-done | bytes 2097168 | tf_op jit(solution)/shard_map/all_gather | solution.py:62
  371.3 3.6 convolution_bitcast_fusion.2
  374.9 0.3 copy.64
  375.2 0.4 reshape.80
  375.6 1.9 fusion.12
  377.5 9.1 %broadcast_multiply_fusion = f32[2,16,256,256]{3,2,1,0:T(8,128)} fusion(f32[2,16,64,256]{3,2,1,0:T(8,128)S(1)} %fusion.12, f32[256,64]{0,1:T(8,128)S(1)} %copy-done), kind=kOutput, calls=%fused_computation.13 | convolution fusion | flops 1612709888 | bytes 10551296 | tf_op jit(solution)/shard_map/ia,pmao->pmio/dot_general | solution.py:67
  386.5 8.7 %copy.65 = f32[2,2,8,256,256]{4,3,2,1,0:T(8,128)} copy(f32[2,2,8,256,256]{3,4,2,1,0:T(8,128)} %bitcast.75) | data formatting | bytes 16777216 | tf_op jit(solution)/shard_map/mul | solution.py:69
  395.3 10.6 %sub.18 = f32[2,2,8,256,256]{4,3,2,1,0:T(8,128)} subtract(f32[2,2,8,256,256]{4,3,2,1,0:T(8,128)} %param.10, f32[2,2,8,256,256]{4,3,2,1,0:T(8,128)} %copy.65) | non-fusion elementwise | flops 2097152 | bytes 25165824 | tf_op jit(solution)/shard_map/sub | solution.py:69
  (11 shorter events, 0.1 us)
Async XLA Ops:
  7.2 107.1 %copy-start = (f32[256,64]{0,1:T(8,128)S(1)}, f32[256,64]{0,1:T(8,128)}, u32[]{:S(2)}) copy-start(f32[256,64]{0,1:T(8,128)} %param.12) | copy-start | bytes 196612
  23.0 41.3 %all-to-all-start.1 = ((bf16[2,1,2048,256]{3,0,1,2:T(2,128)(2,1)}), bf16[2,1,2048,256]{3,0,1,2:T(2,128)(2,1)S(1)}, u32[]{:S(2)}, u32[]{:S(2)}) async-start(bf16[2,1,2048,256]{3,0,1,2:T(2,128)(2,1)} %copy.53), calls=%async_computation.1 | async-start | bytes 4194304 | tf_op jit(solution)/shard_map/all_to_all | solution.py:34
  64.3 35.5 %all-to-all-start = ((bf16[2,1,2048,256]{3,0,1,2:T(2,128)(2,1)}), bf16[2,1,2048,256]{3,0,1,2:T(2,128)(2,1)}, u32[]{:S(2)}, u32[]{:S(2)}) async-start(bf16[2,1,2048,256]{3,0,1,2:T(2,128)(2,1)} %copy.50), calls=%async_computation | async-start | bytes 4194304 | tf_op jit(solution)/shard_map/all_to_all | solution.py:37
  70.1 235.5 %reduce-scatter.2.cloned.1.call-start = ((), (), s32[]{:S(2)}) async-start(), calls=%async_computation.3 | async-start | bytes 2162688 | tf_op jit(solution)/shard_map/reduce_scatter | solution.py:51
  107.8 0.8 copy-start.1
  116.3 0.7 copy-start.4
  117.0 188.7 %copy-start.3 = (f32[8,8,128]{2,1,0:T(8,128)S(1)}, f32[8,8,128]{2,1,0:T(8,128)}, u32[]{:S(2)}) copy-start(f32[8,8,128]{2,1,0:T(8,128)} %param.15) | copy-start | bytes 98308
  117.0 189.5 %copy-start.2 = (f32[2,8,8,128]{3,2,1,0:T(8,128)S(1)}, f32[2,8,8,128]{3,2,1,0:T(8,128)}, u32[]{:S(2)}) copy-start(f32[2,8,8,128]{3,2,1,0:T(8,128)} %param.14) | copy-start | bytes 196612
  120.6 250.7 %all-gather.2.cloned.1.call-start = ((), (), s32[]{:S(2)}) async-start(), calls=%async_computation.4 | async-start | bytes 2162688 | tf_op jit(solution)/shard_map/all_gather | solution.py:62
Sparse Core Ops, SparseCore 0:
  120.7 184.9 reduce-scatter.1
  309.0 62.2 all-gather.1
where the time goes:
time: 413 us
  waiting for transfers between devices  291 us (70%)
  local copies, waits for them, and re-layouts  43.2 us (10%)
  matrix products  33 us (8%)
  starting transfers between devices  17.2 us (4%)
  between operations  14.2 us (3%)
  other arithmetic  14.1 us (3%)
    reduce_scatter x1, waiting for transfers between devices, local(): lax.psum_scatter(partial_core, 'wide', scatter_dimension=3, tiled=True)  185 us
    all_gather x1, waiting for transfers between devices, local(): lax.all_gather(core_step, 'wide', axis=3, tiled=True)  62.1 us
    all_to_all x1, waiting for transfers between devices, local(): lax.all_to_all(arrange(out_grads), ('wide', 'narrow'), split_axis=2, conc...  29.5 us
    reshape x2, local copies, waits for them, and re-layouts, arrange(): source.reshape(2, sample_rows, wide_count * narrow_count * local_modes, w...  28 us
    all_to_all x1, waiting for transfers between devices, local(): lax.all_to_all(arrange(spectra), ('wide', 'narrow'), split_axis=2, concat...  14.4 us
    all_to_all x1, starting transfers between devices, local(): lax.all_to_all(arrange(spectra), ('wide', 'narrow'), split_axis=2, concat...  11.2 us
    sub x1, other arithmetic, local(): new_weights = weights - 0.3 * change  10.6 us
    dot_general x1, matrix products, local(): jnp.einsum('ia,pmao->pmio', in_factor, left_part, precision=highest)  9.08 us
  transfers between devices with their start and end apart: 4, of which 4 were waited for; matrix products, arithmetic and copies ran while one was open for 4% of the time, Pallas kernels for 0%

commit v1 on v0

--- a/solution.py
+++ b/solution.py
@@ -1,10 +1,27 @@
+import functools
 import jax
 import jax.numpy as jnp
 from jax import lax
 from jax.sharding import PartitionSpec as P
+from jax.lax import all_to_all, axis_size
 
 STEP = 1000
 highest = lax.Precision.HIGHEST
+
+
+def step_on_shapes(a0, axis_name):
+    return jnp.concatenate(
+        all_to_all(
+            jnp.stack(axis_size(axis_name) * [a0], axis=0),
+            concat_axis=0,
+            split_axis=0,
+            axis_name=axis_name,
+        ),
+        axis=3,
+    )
+
+
+process_heaps = functools.partial(step_on_shapes, axis_name="wide")
 
 
 def local(
@@ -56,12 +73,7 @@
     first_scale = 1.0 / (1.0 - 0.9**STEP)
     second_scale = 1.0 / (1.0 - 0.999**STEP)
     core_step = new_first * first_scale / (jnp.sqrt(new_second * second_scale) + 1e-08)
-    expanded = jnp.einsum(
-        "xr,prmk->pxmk",
-        mine_rows,
-        lax.all_gather(core_step, "wide", axis=3, tiled=True),
-        precision=highest,
-    )
+    expanded = jnp.einsum("xr,prmk->pxmk", mine_rows, process_heaps(core_step), precision=highest)
     expanded = expanded.reshape(2, local_modes, rank_in, rank_out)
     left_part = jnp.einsum("pmac,oc->pmao", expanded, out_factor, precision=highest)
     change = jnp.einsum("ia,pmao->pmio", in_factor, left_part, precision=highest)

time: 413 us -> 377 us (0.913)
  waiting for transfers between devices: 291 us -> 250 us
    all_gather x1 -> x0, waiting for transfers between devices: 62.1 us -> none  [local(): lax.all_gather(core_step, 'wide', axis=3, tiled=True)]
    all_to_all x0 -> x1, waiting for transfers between devices: none -> 18.1 us  [step_on_shapes(): all_to_all(jnp.stack(axis_size(axis_name) * [a0], axis=0), concat_axis=0,...]
  transfers between devices with their start and end apart: 4 -> 4, of which waited for: 4 -> 4; matrix products, arithmetic and copies ran while one was open for 4% -> 5% of each run, Pallas kernels for 0% -> 0%
where the time goes in v1:
time: 377 us; the launch traced here: 375 us
  waiting for transfers between devices  250 us (66%)
  local copies, waits for them, and re-layouts  44.8 us (12%)
  matrix products  31.4 us (8%)
  starting transfers between devices  21.2 us (6%)
  between operations  14.2 us (4%)
  other arithmetic  13.5 us (4%)
    reduce_scatter x1, waiting for transfers between devices, local(): lax.psum_scatter(partial_core, 'wide', scatter_dimension=3, tiled=True)  188 us
    all_to_all x1, waiting for transfers between devices, local(): lax.all_to_all(arrange(out_grads), ('wide', 'narrow'), split_axis=2, conc...  29.5 us
    reshape x2, local copies, waits for them, and re-layouts, arrange(): source.reshape(2, sample_rows, wide_count * narrow_count * local_modes, w...  28 us
    all_to_all x1, waiting for transfers between devices, step_on_shapes(): all_to_all(jnp.stack(axis_size(axis_name) * [a0], axis=0), concat_axis=0,...  18.1 us
    all_to_all x1, waiting for transfers between devices, local(): lax.all_to_all(arrange(spectra), ('wide', 'narrow'), split_axis=2, concat...  14.4 us
    all_to_all x1, starting transfers between devices, local(): lax.all_to_all(arrange(spectra), ('wide', 'narrow'), split_axis=2, concat...  11.2 us
    sub x1, other arithmetic, local(): new_weights = weights - 0.3 * change  10.6 us
    dot_general x1, matrix products, local(): jnp.einsum('ia,pmao->pmio', in_factor, left_part, precision=highest)  9.08 us
  transfers between devices with their start and end apart: 4, of which 4 were waited for; matrix products, arithmetic and copies ran while one was open for 5% of the time, Pallas kernels for 0%

profile of v1, /device:TPU:0, one launch (start us, length us, event | category | flops | bytes accessed | tf_op | source)
XLA Modules:
  0.0 375.3 jit_solution(3452709790436360612)
XLA Ops:
  7.2 1.8 copy.52
  9.0 14.0 %copy.53 = bf16[2,1,2048,256]{3,0,1,2:T(2,128)(2,1)} copy(bf16[2,1,2048,256]{3,2,0,1:T(8,128)(2,1)S(1)} %bitcast.83) | data formatting | bytes 4194304 | tf_op jit(solution)/shard_map/reshape | solution.py:48
  23.0 11.2 %all-to-all-start.1 = ((bf16[2,1,2048,256]{3,0,1,2:T(2,128)(2,1)}), bf16[2,1,2048,256]{3,0,1,2:T(2,128)(2,1)S(1)}, u32[]{:S(2)}, u32[]{:S(2)}) async-start(bf16[2,1,2048,256]{3,0,1,2:T(2,128)(2,1)} %copy.53), calls=%async_computation.1 | async-start | bytes 4194304 | tf_op jit(solution)/shard_map/all_to_all | solution.py:51
  34.2 1.8 copy.49
  36.0 14.0 %copy.50 = bf16[2,1,2048,256]{3,0,1,2:T(2,128)(2,1)} copy(bf16[2,1,2048,256]{3,2,0,1:T(8,128)(2,1)S(1)} %bitcast.84) | data formatting | bytes 4194304 | tf_op jit(solution)/shard_map/reshape | solution.py:48
  49.9 14.4 %all-to-all-done.1 = bf16[2,1,2048,256]{3,0,1,2:T(2,128)(2,1)S(1)} async-done(((bf16[2,1,2048,256]{3,0,1,2:T(2,128)(2,1)}), bf16[2,1,2048,256]{3,0,1,2:T(2,128)(2,1)S(1)}, u32[]{:S(2)}, u32[]{:S(2)}) %all-to-all-start.1) | async-done | bytes 2097184 | tf_op jit(solution)/shard_map/all_to_all | solution.py:51
  64.3 5.8 %all-to-all-start = ((bf16[2,1,2048,256]{3,0,1,2:T(2,128)(2,1)}), bf16[2,1,2048,256]{3,0,1,2:T(2,128)(2,1)}, u32[]{:S(2)}, u32[]{:S(2)}) async-start(bf16[2,1,2048,256]{3,0,1,2:T(2,128)(2,1)} %copy.50), calls=%async_computation | async-start | bytes 4194304 | tf_op jit(solution)/shard_map/all_to_all | solution.py:54
  70.1 0.2 reduce-scatter.2.cloned.1.call-start
  70.3 29.5 %all-to-all-done = bf16[2,1,2048,256]{3,0,1,2:T(2,128)(2,1)} async-done(((bf16[2,1,2048,256]{3,0,1,2:T(2,128)(2,1)}), bf16[2,1,2048,256]{3,0,1,2:T(2,128)(2,1)}, u32[]{:S(2)}, u32[]{:S(2)}) %all-to-all-start) | async-done | bytes 2097184 | tf_op jit(solution)/shard_map/all_to_all | solution.py:54
  99.8 7.4 %convolution_bitcast_fusion = f32[2,2,16,256,256]{3,4,0,1,2:T(8,128)S(1)} fusion(bf16[2,128,16,256,1]{3,0,2,1,4:T(2,128)(2,1)S(1)} %bitcast.82, bf16[2,128,16,256,1]{3,0,2,1,4:T(2,128)(2,1)} %bitcast.4), kind=kOutput, calls=%fused_computation | convolution fusion | flops 1073741824 | bytes 20971520 | tf_op jit(solution)/shard_map/pbmi,qbmo->pqmio/dot_general | solution.py:58
  107.2 0.6 fusion.4
  107.8 0.6 fusion.6
  108.6 5.6 %fusion = f32[2,16,256,64]{2,3,1,0:T(8,128)S(1)} fusion(f32[1,16,256,256]{2,3,1,0:T(8,128)S(1)} %fusion.4, f32[1,16,256,256]{2,3,1,0:T(8,128)S(1)} %fusion.6, f32[256,64]{0,1:T(8,128)S(1)} %copy-done.1), kind=kOutput, calls=%fused_computation.1 | convolution fusion | flops 1612709888 | bytes 10551296 | tf_op jit(solution)/shard_map/pmio,oc->pmic/dot_general | solution.py:62
  114.2 2.0 convolution_bitcast_fusion.3
  116.3 0.3 copy.60
  116.6 0.4 reshape.87
  117.0 3.5 convolution_bitcast_fusion.1
  120.6 188.3 %reduce-scatter.2.cloned.1.call-done = f32[2,8,8,128]{3,1,2,0:T(8,128)} async-done(((f32[2,8,8,4096]{3,1,2,0:T(8,128)}), f32[2,8,8,128]{3,1,2,0:T(8,128)}) %reduce-scatter.2.cloned.1.call-update) | async-done | bytes 65552 | tf_op jit(solution)/shard_map/reduce_scatter | solution.py:68
  308.8 0.8 sqrt_add_fusion
  309.7 0.9 broadcast_divide_fusion
  310.5 1.6 stack.5
  312.1 4.0 %all-to-all-start.2 = ((f32[32,2,8,8,128]{4,2,3,1,0:T(8,128)}), f32[32,2,8,8,128]{4,2,3,1,0:T(8,128)S(1)}, u32[]{:S(2)}, u32[]{:S(2)}) async-start(f32[32,2,8,8,128]{4,2,3,1,0:T(8,128)} %stack.5), calls=%async_computation.3 | async-start | bytes 4194304 | tf_op jit(solution)/shard_map/all_to_all | solution.py:14
  316.1 0.6 copy.68
  316.7 0.6 copy.67
  317.4 18.1 %all-to-all-done.2 = f32[32,2,8,8,128]{4,2,3,1,0:T(8,128)S(1)} async-done(((f32[32,2,8,8,128]{4,2,3,1,0:T(8,128)}), f32[32,2,8,8,128]{4,2,3,1,0:T(8,128)S(1)}, u32[]{:S(2)}, u32[]{:S(2)}) %all-to-all-start.2) | async-done | bytes 2097184 | tf_op jit(solution)/shard_map/all_to_all | solution.py:14
  335.5 2.0 convolution_bitcast_fusion.2
  337.5 0.3 copy.65
  337.8 0.4 reshape.90
  338.2 1.9 fusion.14
  340.0 9.1 %broadcast_multiply_fusion = f32[2,16,256,256]{3,2,1,0:T(8,128)} fusion(f32[2,16,64,256]{3,2,1,0:T(8,128)S(1)} %fusion.14, f32[256,64]{0,1:T(8,128)S(1)} %copy-done), kind=kOutput, calls=%fused_computation.13 | convolution fusion | flops 1612709888 | bytes 10551296 | tf_op jit(solution)/shard_map/ia,pmao->pmio/dot_general | solution.py:79
  349.1 8.7 %copy.66 = f32[2,2,8,256,256]{4,3,2,1,0:T(8,128)} copy(f32[2,2,8,256,256]{3,4,2,1,0:T(8,128)} %bitcast.81) | data formatting | bytes 16777216 | tf_op jit(solution)/shard_map/mul | solution.py:81
  357.8 10.6 %sub.18 = f32[2,2,8,256,256]{4,3,2,1,0:T(8,128)} subtract(f32[2,2,8,256,256]{4,3,2,1,0:T(8,128)} %param.10, f32[2,2,8,256,256]{4,3,2,1,0:T(8,128)} %copy.66) | non-fusion elementwise | flops 2097152 | bytes 25165824 | tf_op jit(solution)/shard_map/sub | solution.py:81
  (11 shorter events, 0.3 us)
Async XLA Ops:
  7.2 107.1 %copy-start = (f32[256,64]{0,1:T(8,128)S(1)}, f32[256,64]{0,1:T(8,128)}, u32[]{:S(2)}) copy-start(f32[256,64]{0,1:T(8,128)} %param.12) | copy-start | bytes 196612
  23.0 41.3 %all-to-all-start.1 = ((bf16[2,1,2048,256]{3,0,1,2:T(2,128)(2,1)}), bf16[2,1,2048,256]{3,0,1,2:T(2,128)(2,1)S(1)}, u32[]{:S(2)}, u32[]{:S(2)}) async-start(bf16[2,1,2048,256]{3,0,1,2:T(2,128)(2,1)} %copy.53), calls=%async_computation.1 | async-start | bytes 4194304 | tf_op jit(solution)/shard_map/all_to_all | solution.py:51
  64.3 35.5 %all-to-all-start = ((bf16[2,1,2048,256]{3,0,1,2:T(2,128)(2,1)}), bf16[2,1,2048,256]{3,0,1,2:T(2,128)(2,1)}, u32[]{:S(2)}, u32[]{:S(2)}) async-start(bf16[2,1,2048,256]{3,0,1,2:T(2,128)(2,1)} %copy.50), calls=%async_computation | async-start | bytes 4194304 | tf_op jit(solution)/shard_map/all_to_all | solution.py:54
  70.1 238.7 %reduce-scatter.2.cloned.1.call-start = ((), (), s32[]{:S(2)}) async-start(), calls=%async_computation.4 | async-start | bytes 2162688 | tf_op jit(solution)/shard_map/reduce_scatter | solution.py:68
  107.8 0.8 copy-start.1
  116.3 0.7 copy-start.4
  117.0 191.9 %copy-start.3 = (f32[8,8,128]{2,1,0:T(8,128)S(1)}, f32[8,8,128]{2,1,0:T(8,128)}, u32[]{:S(2)}) copy-start(f32[8,8,128]{2,1,0:T(8,128)} %param.15) | copy-start | bytes 98308
  117.0 192.6 %copy-start.2 = (f32[2,8,8,128]{3,2,1,0:T(8,128)S(1)}, f32[2,8,8,128]{3,2,1,0:T(8,128)}, u32[]{:S(2)}) copy-start(f32[2,8,8,128]{3,2,1,0:T(8,128)} %param.14) | copy-start | bytes 196612
  312.1 23.4 %all-to-all-start.2 = ((f32[32,2,8,8,128]{4,2,3,1,0:T(8,128)}), f32[32,2,8,8,128]{4,2,3,1,0:T(8,128)S(1)}, u32[]{:S(2)}, u32[]{:S(2)}) async-start(f32[32,2,8,8,128]{4,2,3,1,0:T(8,128)} %stack.5), calls=%async_computation.3 | async-start | bytes 4194304 | tf_op jit(solution)/shard_map/all_to_all | solution.py:14
Sparse Core Ops, SparseCore 0:
  120.7 188.1 reduce-scatter.1
